TPU v7x, 32 devices: a whole 2x2x4 slice. The times are simulated.
32 devices in a mesh: ens: 2 (over y), wide: 4 (over z), lev: 2 (over x), fld: 2 (over core).
Axes of the slice: x: 2, y: 2, z: 4, core: 2. Of those that a mesh axis runs over, the one named last changes fastest.
Arguments:
- fourier_input_rows: bfloat16 [4, 1280, 4, 4, 256], P('ens', 'wide', None, 'fld', 'lev'), parts along dimension 0, may hold values from -6 to 6
- legendre: bfloat16 [4, 1280, 1280], P('wide', ('lev', 'fld')), may hold values from -0.15625 to 0.15625
- slot_wave: int32 [4], P('wide'), may hold values from 0 to 1279, as said below
- to_modes: bfloat16 [128, 128], replicated, may hold values from -0.5 to 0.5
- from_modes: bfloat16 [128, 128], replicated, may hold values from -0.5 to 0.5
- mode_rate: float32 [128], replicated, may hold values from 0.05 to 5
Outputs:
- fourier_out: bfloat16 [4, 1280, 4, 4, 256], P('ens', 'wide', None, 'fld', 'lev'), parts along dimension 0
- spectral: bfloat16 [8, 1280, 4, 256], P(('ens', 'wide'), None, 'fld', 'lev'), parts along dimension 0
There are 2 independent parts, one for each index of `ens`. A program takes and returns all parts, laid end to end along the dimension named above; an argument that names none is the same for every part. Nothing has to cross between parts.
Inputs may be any that keep to these rules, and one draw needn't show every extreme that they name: `slot_wave`: the wavenumbers of the slots are distinct; one slot holds 0 and one holds 1279.
All inputs are finite; a program needn't handle non-finite values.
Results may differ from a plain program's by a relative error of at most 0.0065.
Values may be sent and summed in bfloat16 or wider, within the bound.
A program may use at most 64 MiB of HBM per device.

v0:
```python
import math
import jax
import jax.numpy as jnp
from jax import lax
from jax.sharding import PartitionSpec as P


def latitude_weights(count):
    position = jnp.arange(count, dtype=jnp.float32)
    return jnp.sin(math.pi * (position + 0.5) / (2 * count))


def project(level_grid, degree_real, weight_rows, rate_rows, degree_total):
    projected = jnp.einsum(
        "kl,snflr->snfkr", weight_rows, level_grid, preferred_element_type=jnp.float32
    )
    factor = 1.0 + degree_real[:, None] * (degree_real[:, None] + 1.0) * rate_rows[None, :] / (
        degree_total * degree_total
    )
    return (projected / factor[None, :, None, :, None]).astype(jnp.bfloat16)


def shards(fourier_input_rows, legendre, slot_wave, to_modes, from_modes, mode_rate):
    wave_rows = lax.all_to_all(fourier_input_rows, "wide", split_axis=2, concat_axis=1, tiled=True)
    half_count = wave_rows.shape[1]
    slot_count = wave_rows.shape[2]
    field_count = wave_rows.shape[3]
    column_count = wave_rows.shape[4]
    degree_count = legendre.shape[1] * lax.axis_size(("lev", "fld"))
    weights = latitude_weights(half_count)[:, None, None, None]
    north_half = wave_rows[0].astype(jnp.float32)
    south_half = wave_rows[1].astype(jnp.float32)
    symmetric = (weights * (north_half + south_half)).astype(jnp.bfloat16)
    antisym = (weights * (north_half - south_half)).astype(jnp.bfloat16)
    paired = jnp.concatenate((symmetric, antisym), axis=3)

    def direct_rows(section, first_row):
        row_count = section.shape[1]
        degree = first_row + jnp.arange(row_count, dtype=jnp.int32)
        relative = degree[None, :] - slot_wave[:, None]
        product = jnp.einsum("snj,jsfc->snfc", section, paired, preferred_element_type=jnp.float32)
        is_even = (relative % 2 == 0)[:, :, None, None]
        is_live = (relative >= 0)[:, :, None, None]
        picked = jnp.where(is_even, product[..., :column_count], product[..., column_count:])
        return jnp.where(is_live, picked, jnp.zeros_like(picked))

    full_table = lax.all_gather(legendre, ("lev", "fld"), axis=1, tiled=True)
    block_rows = 128
    block_count = degree_count // block_rows

    def direct_step(block_index, buffer):
        first_row = block_index * block_rows
        section = lax.dynamic_slice_in_dim(full_table, first_row, block_rows, 1)
        result = direct_rows(section, first_row).astype(jnp.bfloat16)
        return lax.dynamic_update_slice_in_dim(buffer, result, first_row, 1)

    initial_raw = jnp.zeros((slot_count, degree_count, field_count, column_count), jnp.bfloat16)
    raw_spectral = lax.fori_loop(0, block_count, direct_step, initial_raw)
    own_levels = column_count // 2
    first_level = lax.axis_index("lev") * own_levels
    degree_real = jnp.arange(degree_count, dtype=jnp.float32)
    all_levels = lax.all_gather(raw_spectral, "lev", axis=3, tiled=True)
    level_count = all_levels.shape[3] // 2
    level_grid = all_levels.reshape(slot_count, degree_count, field_count, level_count, 2)
    weight_rows = lax.dynamic_slice_in_dim(to_modes, first_level, own_levels, 0)
    rate_rows = lax.dynamic_slice_in_dim(mode_rate, first_level, own_levels, 0)
    own_modes = project(level_grid, degree_real, weight_rows, rate_rows, degree_count).reshape(
        slot_count, degree_count, field_count, column_count
    )
    mode_values = lax.all_gather(own_modes, "lev", axis=3, tiled=True).reshape(
        slot_count, degree_count, field_count, level_count, 2
    )
    back_rows = lax.dynamic_slice_in_dim(from_modes, first_level, own_levels, 0)
    spectral = jnp.einsum(
        "lk,snfkr->snflr", back_rows, mode_values, preferred_element_type=jnp.float32
    )
    spectral = spectral.astype(jnp.bfloat16).reshape(
        slot_count, degree_count, field_count, column_count
    )

    def inverse_rows(running, section, first_row):
        row_count = section.shape[1]
        degree = first_row + jnp.arange(row_count, dtype=jnp.int32)
        relative = degree[None, :] - slot_wave[:, None]
        spec_rows = lax.dynamic_slice_in_dim(spectral, first_row, row_count, 1)
        even_mask = ((relative >= 0) & (relative % 2 == 0))[:, :, None, None]
        odd_mask = ((relative >= 0) & (relative % 2 == 1))[:, :, None, None]
        empty_rows = jnp.zeros_like(spec_rows)
        parity_split = jnp.concatenate(
            (
                jnp.where(even_mask, spec_rows, empty_rows),
                jnp.where(odd_mask, spec_rows, empty_rows),
            ),
            axis=3,
        )
        return running + jnp.einsum(
            "snj,snfc->jsfc", section, parity_split, preferred_element_type=jnp.float32
        )

    initial_sum = jnp.zeros((half_count, slot_count, field_count, 2 * column_count), jnp.float32)

    def inverse_step(block_index, running):
        first_row = block_index * block_rows
        section = lax.dynamic_slice_in_dim(full_table, first_row, block_rows, 1)
        return inverse_rows(running, section, first_row)

    running = lax.fori_loop(0, block_count, inverse_step, initial_sum)
    even_sum = running[..., :column_count]
    odd_sum = running[..., column_count:]
    fourier_wave = jnp.stack((even_sum + odd_sum, even_sum - odd_sum), axis=0).astype(jnp.bfloat16)
    fourier_out = lax.all_to_all(fourier_wave, "wide", split_axis=1, concat_axis=2, tiled=True)
    return (fourier_out, spectral)


def solution(mesh):
    in_specs = (
        P("ens", "wide", None, "fld", "lev"),
        P("wide", ("lev", "fld"), None),
        P("wide"),
        P(),
        P(),
        P(),
    )
    out_specs = (P("ens", "wide", None, "fld", "lev"), P(("ens", "wide"), None, "fld", "lev"))
    return jax.shard_map(shards, mesh=mesh, in_specs=in_specs, out_specs=out_specs, check_vma=False)
```

profile of v0, /device:TPU:0, one launch (start us, length us, event | category | flops | bytes accessed | tf_op | source)
XLA Modules:
  0.0 206.5 jit_solution(15960541568794821746)
XLA Ops:
  7.2 0.7 all-gather.4.cloned.1.call-update
  7.9 3.3 %copy.24 = bf16[2,320,4,2,128]{4,3,1,0,2:T(2,128)(2,1)} copy(bf16[2,320,4,2,128]{4,3,2,1,0:T(2,128)(2,1)} %param.10) | data formatting | bytes 2621440 | tf_op args[0]
  11.2 6.3 %all-to-all-start = ((bf16[2,320,4,2,128]{4,3,1,0,2:T(2,128)(2,1)}), bf16[2,320,4,2,128]{4,3,1,0,2:T(2,128)(2,1)S(1)}, u32[]{:S(2)}, u32[]{:S(2)}) async-start(bf16[2,320,4,2,128]{4,3,1,0,2:T(2,128)(2,1)} %copy.24), calls=%async_computation | async-start | bytes 2621440 | tf_op jit(solution)/shard_map/all_to_all | solution.py:24
  17.6 31.3 %all-to-all-done = bf16[2,320,4,2,128]{4,3,1,0,2:T(2,128)(2,1)S(1)} async-done(((bf16[2,320,4,2,128]{4,3,1,0,2:T(2,128)(2,1)}), bf16[2,320,4,2,128]{4,3,1,0,2:T(2,128)(2,1)S(1)}, u32[]{:S(2)}, u32[]{:S(2)}) %all-to-all-start) | async-done | bytes 1310752 | tf_op jit(solution)/shard_map/all_to_all | solution.py:24
  48.8 0.9 convert_add_fusion
  50.3 21.4 %while.31 = (s32[]{:T(128)}, bf16[1,1280,2,128]{3,1,2,0:T(8,128)(2,1)S(1)}, s32[1]{0:T(128)}, bf16[1,1280,1280]{2,1,0:T(8,128)(2,1)}, bf16[1280,1,2,256]{3,0,2,1...) while((s32[]{:T(128)}, bf16[1,1280,2,128]{3,1,2,0:T(8,128)(2,1)S(1)}, s32[1]{0:T(128)}, ...), condition=%wide.region_1.2_spmd, body=%wide.region_0.1_spmd.sunk | while | flops 167839616 | bytes 1967515 | solution.py:58
  50.4 1.3 fusion.47
  52.5 1.3 fusion.47
  54.6 1.3 fusion.47
  56.8 1.3 fusion.47
  58.9 1.3 fusion.47
  61.1 1.3 fusion.47
  63.2 1.3 fusion.47
  65.3 1.3 fusion.47
  67.5 1.3 fusion.47
  69.6 1.3 fusion.47
  71.8 0.8 copy-done.1
  72.9 23.2 %all-gather.6.cloned.1.call-done = bf16[1,1280,2,256]{3,1,2,0:T(8,128)(2,1)} async-done(((bf16[1,1280,2,128]{3,1,2,0:T(8,128)(2,1)}), bf16[1,1280,2,256]{3,1,2,0:T(8,128)(2,1)}) %all-gather.6.cloned.1.call-update) | async-done | bytes 1310736 | tf_op jit(solution)/shard_map/all_gather | solution.py:62
  96.1 3.6 %copy.27 = bf16[1,1280,2,256]{1,2,3,0:T(2,128)(2,1)S(1)} copy(bf16[1,1280,2,256]{3,1,2,0:T(8,128)(2,1)} %all-gather.6.cloned.1.call-done) | data formatting | bytes 2621440 | tf_op jit(solution)/shard_map/all_gather | solution.py:62
  100.1 1.5 copy.29
  101.6 24.4 %all-gather.8.cloned.1.call-done = bf16[1,1280,2,256]{1,2,0,3:T(2,128)(2,1)} async-done(((bf16[1,1280,2,128]{1,2,0,3:T(2,128)(2,1)}), bf16[1,1280,2,256]{1,2,0,3:T(2,128)(2,1)}) %all-gather.8.cloned.1.call-update) | async-done | bytes 1310736 | tf_op jit(solution)/shard_map/all_gather | solution.py:70
  126.0 1.6 fusion.22
  127.7 0.7 copy.32
  128.4 25.0 %while.32 = (s32[]{:T(128)}, f32[1280,1,2,256]{0,3,2,1:T(8,128)S(1)}, s32[1]{0:T(128)}, bf16[1,1280,2,128]{1,2,3,0:T(2,128)(2,1)S(1)}, bf16[1,1280,1280]{2,1,0:T...) while((s32[]{:T(128)}, f32[1280,1,2,256]{0,3,2,1:T(8,128)S(1)}, s32[1]{0:T(128)}, ...), condition=%wide.region_3.4_spmd.clone, body=%wide.region_2.3_spmd.clone.sunk | while | flops 169412864 | bytes 6029989 | solution.py:107
  128.4 0.7 compare_and_fusion.3
  129.1 1.7 fusion.51
  130.9 0.7 compare_and_fusion.3
  131.6 1.7 fusion.51
  133.4 0.7 compare_and_fusion.3
  134.1 1.7 fusion.51
  135.9 0.7 compare_and_fusion.3
  136.6 1.7 fusion.51
  138.4 0.7 compare_and_fusion.3
  139.1 1.7 fusion.51
  140.9 0.7 compare_and_fusion.3
  141.6 1.7 fusion.51
  144.1 1.7 fusion.51
  145.9 0.7 compare_and_fusion.3
  146.6 1.7 fusion.51
  149.1 1.7 fusion.51
  151.6 1.7 fusion.51
  153.4 3.1 %copy.34 = f32[1280,1,2,256]{3,2,0,1:T(2,128)} copy(f32[1280,1,2,256]{0,3,2,1:T(8,128)S(1)} %get-tuple-element.269) | data formatting | bytes 5242880 | tf_op jit(solution)/shard_map/while | solution.py:107
  156.5 2.2 %fusion.30 = (bf16[1,1280,1,2,128]{4,3,0,2,1:T(2,128)(2,1)S(1)}, bf16[1,1280,1,2,128]{4,3,0,2,1:T(2,128)(2,1)S(1)}) fusion(f32[1280,1,2,256]{3,2,0,1:T(2,128)} %copy.34), kind=kLoop, calls=%fused_computation.54 | loop fusion | flops 1310720 | bytes 3932160 | tf_op jit(solution)/shard_map/stack | solution.py:110
  158.7 2.7 %pad_maximum_fusion.1 = bf16[2,1280,1,2,128]{4,3,0,2,1:T(2,128)(2,1)} fusion(bf16[1,1280,1,2,128]{4,3,0,2,1:T(2,128)(2,1)S(1)} %get-tuple-element.334, bf16[1,1280,1,2,128]{4,3,0,2,1:T(2,128)(2,1)S(1)} %get-tuple-element.333), kind=kLoop, calls=%fused_computation.45 | loop fusion | flops 655360 | bytes 2621440 | tf_op jit(solution)/shard_map/stack | solution.py:110
  161.5 4.6 %all-to-all-start.1 = ((bf16[2,1280,1,2,128]{4,3,0,2,1:T(2,128)(2,1)}), bf16[2,1280,1,2,128]{4,3,0,2,1:T(2,128)(2,1)S(1)}, u32[]{:S(2)}, u32[]{:S(2)}) async-start(bf16[2,1280,1,2,128]{4,3,0,2,1:T(2,128)(2,1)} %pad_maximum_fusion.1), calls=%async_computation.1 | async-start | bytes 2621440 | tf_op jit(solution)/shard_map/all_to_all | solution.py:111
  166.1 2.1 %copy.39 = bf16[1,1280,2,128]{3,2,1,0:T(2,128)(2,1)} copy(bf16[1,1280,2,128]{1,2,3,0:T(2,128)(2,1)S(1)} %get-tuple-element.472) | data formatting | bytes 1310720
  168.2 29.2 %all-to-all-done.1 = bf16[2,1280,1,2,128]{4,3,0,2,1:T(2,128)(2,1)S(1)} async-done(((bf16[2,1280,1,2,128]{4,3,0,2,1:T(2,128)(2,1)}), bf16[2,1280,1,2,128]{4,3,0,2,1:T(2,128)(2,1)S(1)}, u32[]{:S(2)}, u32[]{:S(2)}) %all-to-all-start.1) | async-done | bytes 1310752 | tf_op jit(solution)/shard_map/all_to_all | solution.py:111
  197.6 2.4 %copy.38 = bf16[2,320,4,2,128]{4,3,2,1,0:T(2,128)(2,1)} copy(bf16[2,320,4,2,128]{4,1,2,3,0:T(8,128)(2,1)S(1)} %bitcast.88) | data formatting | bytes 2621440
  (66 shorter events, 12.0 us)
Async XLA Ops:
  7.2 92.5 %copy-start = (bf16[128,128]{1,0:T(8,128)(2,1)S(1)}, bf16[128,128]{1,0:T(8,128)(2,1)}, u32[]{:S(2)}) copy-start(bf16[128,128]{1,0:T(8,128)(2,1)} %param.13) | copy-start | bytes 98308
  7.2 43.1 %all-gather.4.cloned.1.call-start = ((), (), s32[]{:S(2)}) async-start(), calls=%async_computation.2 | async-start | bytes 4096000 | tf_op jit(solution)/shard_map/all_gather | solution.py:47
  11.2 37.7 %all-to-all-start = ((bf16[2,320,4,2,128]{4,3,1,0,2:T(2,128)(2,1)}), bf16[2,320,4,2,128]{4,3,1,0,2:T(2,128)(2,1)S(1)}, u32[]{:S(2)}, u32[]{:S(2)}) async-start(bf16[2,320,4,2,128]{4,3,1,0,2:T(2,128)(2,1)} %copy.24), calls=%async_computation | async-start | bytes 2621440 | tf_op jit(solution)/shard_map/all_to_all | solution.py:24
  17.5 78.6 %all-gather.6.cloned.1.call-start = ((), (), s32[]{:S(2)}) async-start(), calls=%async_computation.3 | async-start | bytes 1966080 | tf_op jit(solution)/shard_map/all_gather | solution.py:62
  50.3 22.3 %copy-start.3 = (f32[128]{0:T(128)S(1)}, f32[128]{0:T(128)}, u32[]{:S(2)}) copy-start(f32[128]{0:T(128)} %param.15) | copy-start | bytes 1540
  71.7 0.8 copy-start.1
  72.6 53.4 %all-gather.8.cloned.1.call-start = ((), (), s32[]{:S(2)}) async-start(), calls=%async_computation.4 | async-start | bytes 1966080 | tf_op jit(solution)/shard_map/all_gather | solution.py:70
  100.1 26.0 %copy-start.2 = (bf16[128,128]{1,0:T(8,128)(2,1)S(1)}, bf16[128,128]{1,0:T(8,128)(2,1)}, u32[]{:S(2)}) copy-start(bf16[128,128]{1,0:T(8,128)(2,1)} %param.14) | copy-start | bytes 98308
  161.5 35.9 %all-to-all-start.1 = ((bf16[2,1280,1,2,128]{4,3,0,2,1:T(2,128)(2,1)}), bf16[2,1280,1,2,128]{4,3,0,2,1:T(2,128)(2,1)S(1)}, u32[]{:S(2)}, u32[]{:S(2)}) async-start(bf16[2,1280,1,2,128]{4,3,0,2,1:T(2,128)(2,1)} %pad_maximum_fusion.1), calls=%async_computation.1 | async-start | bytes 2621440 | tf_op jit(solution)/shard_map/all_to_all | solution.py:111
Sparse Core Ops, SparseCore 0:
  9.6 31.9 all-gather.3
  72.7 23.3 all-gather.5
  101.7 24.2 all-gather.7
where the time goes:
time: 208 us; the launch traced here: 207 us
  waiting for transfers between devices  109 us (52%)
  matrix products  32.3 us (16%)
  other arithmetic  21.1 us (10%)
  local copies, waits for them, and re-layouts  18.4 us (9%)
  between operations  13.9 us (7%)
  starting transfers between devices  11 us (5%)
    all_to_all x1, waiting for transfers between devices, shards(): lax.all_to_all(fourier_input_rows, 'wide', split_axis=2, concat_axis=1, t...  31.3 us
    all_to_all x1, waiting for transfers between devices, shards(): lax.all_to_all(fourier_wave, 'wide', split_axis=1, concat_axis=2, tiled=T...  29.2 us
    all_gather x1, waiting for transfers between devices, shards(): lax.all_gather(own_modes, 'lev', axis=3, tiled=True)  24.4 us
    all_gather x1, waiting for transfers between devices, shards(): all_levels = lax.all_gather(raw_spectral, 'lev', axis=3, tiled=True)  23.2 us
    dot_general x10, matrix products, inverse_rows(): jnp.einsum('snj,snfc->jsfc', section, parity_split, preferred_element_typ...  17.2 us
    dot_general x10, matrix products, direct_rows(): jnp.einsum('snj,jsfc->snfc', section, paired, preferred_element_type=jnp....  13.2 us
    unnamed x11, local copies, waits for them, and re-layouts  8.65 us
    and x10, other arithmetic, inverse_rows(): odd_mask = ((relative >= 0) & (relative % 2 == 1))[:, :, None, None]  6.62 us
  transfers between devices with their start and end apart: 5, of which 4 were waited for; matrix products, arithmetic and copies ran while one was open for 3% of the time, Pallas kernels for 0%

commit v1 on v0

--- a/solution.py
+++ b/solution.py
@@ -3,6 +3,19 @@
 import jax.numpy as jnp
 from jax import lax
 from jax.sharding import PartitionSpec as P
+
+
+def tables_trace(x_part, array_axis, view):
+    arr_out, low = (x_part.shape[:array_axis], x_part.shape[array_axis + 1 :])
+    next_value = jnp.moveaxis(x_part.reshape(*arr_out, view, -1, *low), array_axis, 0)
+    return next_value
+
+
+def hold_sizes(z, dim_i):
+    work_now = list(z.shape[1:])
+    work_now[dim_i] *= z.shape[0]
+    a_now = jnp.moveaxis(z, 0, dim_i).reshape(work_now)
+    return a_now
 
 
 def latitude_weights(count):
@@ -108,7 +121,21 @@
     even_sum = running[..., :column_count]
     odd_sum = running[..., column_count:]
     fourier_wave = jnp.stack((even_sum + odd_sum, even_sum - odd_sum), axis=0).astype(jnp.bfloat16)
-    fourier_out = lax.all_to_all(fourier_wave, "wide", split_axis=1, concat_axis=2, tiled=True)
+
+    def follow_members_all_for(xs, shard_axis, buf, block_here):
+        s_next, g_now = (lax.axis_size(shard_axis), lax.axis_index(shard_axis))
+        outer = tables_trace(xs, buf, s_next)
+        pile = [outer[g_now]]
+        for idx in range(1, s_next):
+            passed = outer[(g_now + idx) % s_next]
+            pile.append(
+                lax.ppermute(passed, shard_axis, [(s, (s + idx) % s_next) for s in range(s_next)])
+            )
+        outer = jnp.stack(pile, axis=0)[(g_now - jnp.arange(s_next)) % s_next]
+        after = hold_sizes(outer, block_here)
+        return after
+
+    fourier_out = follow_members_all_for(fourier_wave, "wide", 1, 2)
     return (fourier_out, spectral)
 
 

time: 208 us -> 201 us (0.966)
  the two profiles are of different devices: /device:TPU:0 before, /device:TPU:9 now
where the time goes in v1:
time: 201 us; the launch traced here: 199 us
  waiting for transfers between devices  105 us (52%)
  matrix products  32.3 us (16%)
  other arithmetic  19.3 us (10%)
  local copies, waits for them, and re-layouts  18.8 us (9%)
  between operations  14 us (7%)
  starting transfers between devices  8.48 us (4%)
    all_to_all x1, waiting for transfers between devices, shards(): lax.all_to_all(fourier_input_rows, 'wide', split_axis=2, concat_axis=1, t...  27.4 us
    all_gather x1, waiting for transfers between devices, shards(): all_levels = lax.all_gather(raw_spectral, 'lev', axis=3, tiled=True)  27.1 us
    ppermute x3, waiting for transfers between devices, follow_members_all_for(): lax.ppermute(passed, shard_axis, [(s, (s + idx) % s_next) for s in range(...  25.9 us
    all_gather x1, waiting for transfers between devices, shards(): lax.all_gather(own_modes, 'lev', axis=3, tiled=True)  24.3 us
    dot_general x10, matrix products, inverse_rows(): jnp.einsum('snj,snfc->jsfc', section, parity_split, preferred_element_typ...  17.2 us
    dot_general x10, matrix products, direct_rows(): jnp.einsum('snj,jsfc->snfc', section, paired, preferred_element_type=jnp....  13.2 us
    unnamed x13, local copies, waits for them, and re-layouts  9.4 us
    and x10, other arithmetic, inverse_rows(): odd_mask = ((relative >= 0) & (relative % 2 == 1))[:, :, None, None]  6.62 us
  transfers between devices with their start and end apart: 7, of which 6 were waited for; matrix products, arithmetic and copies ran while one was open for 4% of the time, Pallas kernels for 0%

profile of v1, /device:TPU:9, one launch (start us, length us, event | category | flops | bytes accessed | tf_op | source)
XLA Modules:
  0.0 199.3 jit_solution(1589768890174600567)
XLA Ops:
  7.2 0.7 all-gather.4.cloned.1.call-update
  7.9 3.3 %copy.27 = bf16[2,320,4,2,128]{4,3,1,0,2:T(2,128)(2,1)} copy(bf16[2,320,4,2,128]{4,3,2,1,0:T(2,128)(2,1)} %param.10) | data formatting | bytes 2621440 | tf_op args[0]
  11.2 4.8 %all-to-all-start = ((bf16[2,320,4,2,128]{4,3,1,0,2:T(2,128)(2,1)}), bf16[2,320,4,2,128]{4,3,1,0,2:T(2,128)(2,1)S(1)}, u32[]{:S(2)}, u32[]{:S(2)}) async-start(bf16[2,320,4,2,128]{4,3,1,0,2:T(2,128)(2,1)} %copy.27), calls=%async_computation | async-start | bytes 2621440 | tf_op jit(solution)/shard_map/all_to_all | solution.py:37
  16.0 27.4 %all-to-all-done = bf16[2,320,4,2,128]{4,3,1,0,2:T(2,128)(2,1)S(1)} async-done(((bf16[2,320,4,2,128]{4,3,1,0,2:T(2,128)(2,1)}), bf16[2,320,4,2,128]{4,3,1,0,2:T(2,128)(2,1)S(1)}, u32[]{:S(2)}, u32[]{:S(2)}) %all-to-all-start) | async-done | bytes 1310752 | tf_op jit(solution)/shard_map/all_to_all | solution.py:37
  43.4 0.9 convert_add_fusion
  44.9 21.4 %while.31 = (s32[]{:T(128)}, bf16[1,1280,2,128]{3,1,2,0:T(8,128)(2,1)S(1)}, s32[1]{0:T(128)}, bf16[1,1280,1280]{2,1,0:T(8,128)(2,1)}, bf16[1280,1,2,256]{3,0,2,1...) while((s32[]{:T(128)}, bf16[1,1280,2,128]{3,1,2,0:T(8,128)(2,1)S(1)}, s32[1]{0:T(128)}, ...), condition=%wide.region_1.2_spmd, body=%wide.region_0.1_spmd.sunk | while | flops 167839616 | bytes 1967515 | solution.py:71
  44.9 1.3 fusion.55
  47.0 1.3 fusion.55
  49.2 1.3 fusion.55
  51.3 1.3 fusion.55
  53.5 1.3 fusion.55
  55.6 1.3 fusion.55
  57.7 1.3 fusion.55
  59.9 1.3 fusion.55
  62.0 1.3 fusion.55
  64.2 1.3 fusion.55
  66.3 0.8 copy-done.1
  67.4 27.1 %all-gather.6.cloned.1.call-done = bf16[1,1280,2,256]{3,1,2,0:T(8,128)(2,1)} async-done(((bf16[1,1280,2,128]{3,1,2,0:T(8,128)(2,1)}), bf16[1,1280,2,256]{3,1,2,0:T(8,128)(2,1)}) %all-gather.6.cloned.1.call-update) | async-done | bytes 1310736 | tf_op jit(solution)/shard_map/all_gather | solution.py:75
  94.6 3.6 %copy.30 = bf16[1,1280,2,256]{1,2,3,0:T(2,128)(2,1)S(1)} copy(bf16[1,1280,2,256]{3,1,2,0:T(8,128)(2,1)} %all-gather.6.cloned.1.call-done) | data formatting | bytes 2621440 | tf_op jit(solution)/shard_map/all_gather | solution.py:75
  98.5 1.5 copy.32
  100.1 24.3 %all-gather.8.cloned.1.call-done = bf16[1,1280,2,256]{1,2,0,3:T(2,128)(2,1)} async-done(((bf16[1,1280,2,128]{1,2,0,3:T(2,128)(2,1)}), bf16[1,1280,2,256]{1,2,0,3:T(2,128)(2,1)}) %all-gather.8.cloned.1.call-update) | async-done | bytes 1310736 | tf_op jit(solution)/shard_map/all_gather | solution.py:83
  124.5 1.6 fusion.22
  126.1 0.7 copy.35
  126.8 25.0 %while.32 = (s32[]{:T(128)}, f32[1280,1,2,256]{0,3,2,1:T(8,128)S(1)}, s32[1]{0:T(128)}, bf16[1,1280,2,128]{1,2,3,0:T(2,128)(2,1)S(1)}, bf16[1,1280,1280]{2,1,0:T...) while((s32[]{:T(128)}, f32[1280,1,2,256]{0,3,2,1:T(8,128)S(1)}, s32[1]{0:T(128)}, ...), condition=%wide.region_3.4_spmd.clone, body=%wide.region_2.3_spmd.clone.sunk | while | flops 169412864 | bytes 6029989 | solution.py:120
  127.6 1.7 fusion.59
  130.1 1.7 fusion.59
  132.6 1.7 fusion.59
  135.1 1.7 fusion.59
  136.9 0.7 compare_and_fusion.3
  137.6 1.7 fusion.59
  140.1 1.7 fusion.59
  142.6 1.7 fusion.59
  145.1 1.7 fusion.59
  147.6 1.7 fusion.59
  150.1 1.7 fusion.59
  151.8 2.1 %copy.37 = f32[1280,1,2,256]{3,0,2,1:T(8,128)} copy(f32[1280,1,2,256]{0,3,2,1:T(8,128)S(1)} %get-tuple-element.269) | data formatting | bytes 5242880 | tf_op jit(solution)/shard_map/while | solution.py:120
  154.0 1.9 subtract_convert_fusion
  156.0 1.3 collective-permute-start
  157.3 1.1 collective-permute-start.1
  158.4 1.2 collective-permute-start.2
  159.7 2.1 %copy.44 = bf16[1,1280,2,128]{3,2,1,0:T(2,128)(2,1)} copy(bf16[1,1280,2,128]{1,2,3,0:T(2,128)(2,1)S(1)} %get-tuple-element.475) | data formatting | bytes 1310720
  161.8 2.8 %collective-permute-done = bf16[2,320,1,2,128]{4,1,3,0,2:T(8,128)(2,1)S(1)} collective-permute-done((bf16[2,320,1,2,128]{4,1,3,0,2:T(8,128)(2,1)S(1)}, bf16[2,320,1,2,128]{4,1,3,0,2:T(8,128)(2,1)S(1)}, u32[]{:S(2)}, u32[]{:S(2)}) %collective-permute-start) | collective-permute-done | bytes 327712 | tf_op jit(solution)/shard_map/ppermute | solution.py:132
  164.7 20.2 %collective-permute-done.1 = bf16[2,320,1,2,128]{4,1,3,0,2:T(8,128)(2,1)S(1)} collective-permute-done((bf16[2,320,1,2,128]{4,1,3,0,2:T(8,128)(2,1)S(1)}, bf16[2,320,1,2,128]{4,1,3,0,2:T(8,128)(2,1)S(1)}, u32[]{:S(2)}, u32[]{:S(2)}) %collective-permute-start.1) | collective-permute-done | bytes 327712 | tf_op jit(solution)/shard_map/ppermute | solution.py:132
  184.8 2.9 %collective-permute-done.2 = bf16[2,320,1,2,128]{4,1,3,0,2:T(8,128)(2,1)S(1)} collective-permute-done((bf16[2,320,1,2,128]{4,1,3,0,2:T(8,128)(2,1)S(1)}, bf16[2,320,1,2,128]{4,1,3,0,2:T(8,128)(2,1)S(1)}, u32[]{:S(2)}, u32[]{:S(2)}) %collective-permute-start.2) | collective-permute-done | bytes 327712 | tf_op jit(solution)/shard_map/ppermute | solution.py:132
  187.7 0.7 copy-done.2
  188.4 1.1 maximum_bitcast_fusion.2
  189.6 0.8 gather_fusion
  190.4 2.4 %copy.43 = bf16[2,320,4,2,128]{4,3,2,1,0:T(2,128)(2,1)} copy(bf16[2,320,4,2,128]{4,1,3,0,2:T(8,128)(2,1)S(1)} %bitcast.107) | data formatting | bytes 2621440
  (75 shorter events, 15.9 us)
Async XLA Ops:
  7.2 91.0 %copy-start = (bf16[128,128]{1,0:T(8,128)(2,1)S(1)}, bf16[128,128]{1,0:T(8,128)(2,1)}, u32[]{:S(2)}) copy-start(bf16[128,128]{1,0:T(8,128)(2,1)} %param.13) | copy-start | bytes 98308
  7.2 37.6 %all-gather.4.cloned.1.call-start = ((), (), s32[]{:S(2)}) async-start(), calls=%async_computation.1 | async-start | bytes 4096000 | tf_op jit(solution)/shard_map/all_gather | solution.py:60
  11.2 32.2 %all-to-all-start = ((bf16[2,320,4,2,128]{4,3,1,0,2:T(2,128)(2,1)}), bf16[2,320,4,2,128]{4,3,1,0,2:T(2,128)(2,1)S(1)}, u32[]{:S(2)}, u32[]{:S(2)}) async-start(bf16[2,320,4,2,128]{4,3,1,0,2:T(2,128)(2,1)} %copy.27), calls=%async_computation | async-start | bytes 2621440 | tf_op jit(solution)/shard_map/all_to_all | solution.py:37
  15.9 78.6 %all-gather.6.cloned.1.call-start = ((), (), s32[]{:S(2)}) async-start(), calls=%async_computation.2 | async-start | bytes 1966080 | tf_op jit(solution)/shard_map/all_gather | solution.py:75
  44.9 22.3 %copy-start.4 = (f32[128]{0:T(128)S(1)}, f32[128]{0:T(128)}, u32[]{:S(2)}) copy-start(f32[128]{0:T(128)} %param.15) | copy-start | bytes 1540
  66.3 0.8 copy-start.1
  67.1 57.3 %all-gather.8.cloned.1.call-start = ((), (), s32[]{:S(2)}) async-start(), calls=%async_computation.3 | async-start | bytes 1966080 | tf_op jit(solution)/shard_map/all_gather | solution.py:83
  98.5 26.0 %copy-start.3 = (bf16[128,128]{1,0:T(8,128)(2,1)S(1)}, bf16[128,128]{1,0:T(8,128)(2,1)}, u32[]{:S(2)}) copy-start(bf16[128,128]{1,0:T(8,128)(2,1)} %param.14) | copy-start | bytes 98308
  156.0 8.6 %collective-permute-start = (bf16[2,320,1,2,128]{4,1,3,0,2:T(8,128)(2,1)S(1)}, bf16[2,320,1,2,128]{4,1,3,0,2:T(8,128)(2,1)S(1)}, u32[]{:S(2)}, u32[]{:S(2)}) collective-permute-start(bf16[2,320,1,2,128]{4,1,3,0,2:T(8,128)(2,1)S(1)} %get-tuple-element.336), channel_id=1, source_target_pairs={{0,4},{4,8},{8,12},{12,0},{1,5},{5,9},{9,13},{13,1},{2,6},{6,10},{... | collective-permute-start | bytes 983048 | tf_op jit(solution)/shard_map/ppermute | solution.py:132
  157.3 27.5 %collective-permute-start.1 = (bf16[2,320,1,2,128]{4,1,3,0,2:T(8,128)(2,1)S(1)}, bf16[2,320,1,2,128]{4,1,3,0,2:T(8,128)(2,1)S(1)}, u32[]{:S(2)}, u32[]{:S(2)}) collective-permute-start(bf16[2,320,1,2,128]{4,1,3,0,2:T(8,128)(2,1)S(1)} %get-tuple-element.337), channel_id=1, source_target_pairs={{0,8},{4,12},{8,0},{12,4},{1,9},{5,13},{9,1},{13,5},{2,10},{6,14},... | collective-permute-start | bytes 983048 | tf_op jit(solution)/shard_map/ppermute | solution.py:132
  158.4 29.3 %collective-permute-start.2 = (bf16[2,320,1,2,128]{4,1,3,0,2:T(8,128)(2,1)S(1)}, bf16[2,320,1,2,128]{4,1,3,0,2:T(8,128)(2,1)S(1)}, u32[]{:S(2)}, u32[]{:S(2)}) collective-permute-start(bf16[2,320,1,2,128]{4,1,3,0,2:T(8,128)(2,1)S(1)} %get-tuple-element.338), channel_id=1, source_target_pairs={{0,12},{4,0},{8,4},{12,8},{1,13},{5,1},{9,5},{13,9},{2,14},{6,2},{... | collective-permute-start | bytes 983048 | tf_op jit(solution)/shard_map/ppermute | solution.py:132
  187.7 0.7 copy-start.2
Sparse Core Ops, SparseCore 0:
  9.6 30.8 all-gather.3
  67.3 27.2 all-gather.5
  100.2 24.2 all-gather.7
